TPU v7x, 32 devices: a whole 2x2x4 slice. The times are simulated.
32 devices in a mesh: head: 4 (over x, core), blk: 8 (over z, y).
Axes of the slice: x: 2, y: 2, z: 4, core: 2. Of those that a mesh axis runs over, the one named last changes fastest.
Arguments:
- inputs: bfloat16 [2, 2048, 768], P(None, ('blk', 'head')), may hold values from -6 to 6
- time_embed: float32 [2, 128], replicated, may hold values from -6 to 6
- segments: int32 [2, 2048], P(None, ('blk', 'head')), may hold values from 0 to 15, never falling along the last dimension, each value on 1 to 1280 neighbouring positions
- valid_mask: int32 [2, 2048], P(None, ('blk', 'head')), may hold values from 0 to 1
- teacher: bfloat16 [2, 2048, 768], P(None, ('blk', 'head')), may hold values from -6 to 6
- ada_weight: bfloat16 [128, 4608], P(None, ('head', 'blk')), may hold values from -0.25 to 0.25
- ada_bias: bfloat16 [4608], P(('head', 'blk')), may hold values from -3 to 3
- gain_attn: bfloat16 [768], P(('head', 'blk')), may hold values from 0.5 to 1.5
- qkv_weight: bfloat16 [768, 2304], P(('head', 'blk')), may hold values from -0.21875 to 0.21875
- out_weight: bfloat16 [768, 768], P(('head', 'blk')), may hold values from -3 to 3
- gain_mlp: bfloat16 [768], P(('head', 'blk')), may hold values from 0.5 to 1.5
- up_weight: bfloat16 [768, 3072], P(('head', 'blk')), may hold values from -0.21875 to 0.21875
- up_bias: bfloat16 [3072], P(('head', 'blk')), may hold values from -3 to 3
- down_weight: bfloat16 [3072, 768], P(('head', 'blk')), may hold values from -0.109375 to 0.109375
- down_bias: bfloat16 [768], P(('head', 'blk')), may hold values from -3 to 3
Outputs:
- output: bfloat16 [2, 2048, 768], P(None, ('blk', 'head'))
- loss_value: float32 [], replicated
- grad_input: float32 [2, 2048, 768], P(None, ('blk', 'head'))
- grad_ada_weight: float32 [128, 4608], P(None, ('head', 'blk'))
- grad_ada_bias: float32 [4608], P(('head', 'blk'))
- grad_gain_attn: float32 [768], P(('head', 'blk'))
- grad_qkv_weight: float32 [768, 2304], P(('head', 'blk'))
- grad_out_weight: float32 [768, 768], P(('head', 'blk'))
- grad_gain_mlp: float32 [768], P(('head', 'blk'))
- grad_up_weight: float32 [768, 3072], P(('head', 'blk'))
- grad_up_bias: float32 [3072], P(('head', 'blk'))
- grad_down_weight: float32 [3072, 768], P(('head', 'blk'))
- grad_down_bias: float32 [768], P(('head', 'blk'))
Inputs may be any that keep to these rules, and one draw needn't show every extreme that they name: `segments`: documents are numbered from 0 along each sequence, never falling; a document has 1 to 1280 tokens, and one has exactly that many.
All inputs are finite; a program needn't handle non-finite values.
Results may differ from a plain program's by a relative error of at most 0.019.
Values may be sent and summed in bfloat16 or wider, within the bound.
No kernel may reach another device: no remote copies, remote signals or barrier semaphores. Data moves between devices by JAX's collectives and lax.ppermute only.
A program may use at most 576 MiB of HBM per device.

v0:
```python
from functools import partial
import jax
import jax.numpy as jnp
from jax import lax
from jax.sharding import PartitionSpec as P

HEADS = 12
HEAD_DIM = 64
precise = lax.Precision.HIGHEST


def normalize(hidden):
    average = jnp.mean(hidden, axis=-1, keepdims=True)
    centred = hidden - average
    variance = jnp.mean(centred * centred, axis=-1, keepdims=True)
    inverse = lax.rsqrt(variance + 1e-05)
    return (centred * inverse, inverse)


def norm_back(upstream, normed, inverse):
    first_mean = jnp.mean(upstream, axis=-1, keepdims=True)
    second_mean = jnp.mean(upstream * normed, axis=-1, keepdims=True)
    return inverse * (upstream - first_mean - normed * second_mean)


def split_three(value):
    high_part = value.astype(jnp.bfloat16)
    rest = value - high_part.astype(jnp.float32)
    middle_part = rest.astype(jnp.bfloat16)
    last_part = (rest - middle_part.astype(jnp.float32)).astype(jnp.bfloat16)
    return jnp.stack([high_part, middle_part, last_part], axis=2)


def on_device(
    inputs,
    time_embed,
    segments,
    valid_mask,
    teacher,
    ada_weight,
    ada_bias,
    gain_attn,
    qkv_weight,
    out_weight,
    gain_mlp,
    up_weight,
    up_bias,
    down_weight,
    down_bias,
):
    seq_count, tokens, model_width = inputs.shape
    n_head = lax.axis_size("head")
    n_blk = lax.axis_size("blk")
    length = tokens * n_head * n_blk
    queries = tokens * n_head
    heads_here = HEADS // n_head
    local_width = heads_here * HEAD_DIM
    scale_factor = HEAD_DIM ** (-0.5)
    bf16 = jnp.bfloat16
    f32 = jnp.float32
    blk_here = lax.axis_index("blk")
    all_docs = lax.all_gather(segments, ("head", "blk"), axis=1, tiled=True)
    key_docs = (
        all_docs.reshape(seq_count, n_head, n_blk, tokens)
        .transpose(0, 2, 1, 3)
        .reshape(seq_count, length)
    )
    query_docs = lax.dynamic_slice_in_dim(key_docs, blk_here * queries, queries, 1)
    mask_float = valid_mask.astype(f32)
    count_here = jnp.sum(mask_float)
    gathered = (
        lax.all_gather(qkv_weight, ("head", "blk"), axis=0, tiled=True),
        lax.all_gather(out_weight, ("head", "blk"), axis=0, tiled=True),
        lax.all_gather(up_weight, ("head", "blk"), axis=0, tiled=True),
        lax.all_gather(down_weight, ("head", "blk"), axis=0, tiled=True),
        lax.all_gather(ada_weight, ("head", "blk"), axis=1, tiled=True),
        lax.all_gather(ada_bias, ("head", "blk"), axis=0, tiled=True),
        lax.all_gather(gain_attn, ("head", "blk"), axis=0, tiled=True),
        lax.all_gather(gain_mlp, ("head", "blk"), axis=0, tiled=True),
        lax.all_gather(up_bias, ("head", "blk"), axis=0, tiled=True),
        lax.all_gather(down_bias, ("head", "blk"), axis=0, tiled=True),
    )
    (
        full_qkv,
        full_out,
        full_up,
        full_down,
        full_ada,
        full_ada_bias,
        full_gain_attn,
        full_gain_mlp,
        full_up_bias,
        full_down_bias,
    ) = gathered
    gain_one = full_gain_attn.astype(f32)
    gain_two = full_gain_mlp.astype(f32)
    modulation = jnp.dot(
        time_embed, full_ada.astype(f32), precision=precise
    ) + full_ada_bias.astype(f32)
    pieces = modulation.reshape(seq_count, 6, 1, model_width)
    shift_attn = pieces[:, 0]
    scale_attn = pieces[:, 1]
    gate_attn = pieces[:, 2]
    shift_mlp = pieces[:, 3]
    scale_mlp = pieces[:, 4]
    gate_mlp = pieces[:, 5]
    residual = inputs.astype(f32)
    normed_one, inverse_one = normalize(residual)
    scaled_one = normed_one * gain_one
    entered = (scaled_one * (1.0 + scale_attn) + shift_attn).astype(bf16)
    triple = jnp.einsum("std,df->stf", entered, full_qkv, preferred_element_type=f32).astype(bf16)
    triple = triple.reshape(seq_count, tokens, 3, model_width)
    grouped = lax.all_to_all(triple, "head", split_axis=3, concat_axis=1, tiled=True)
    query_send = grouped[:, :, 0]
    query_heads = query_send.reshape(seq_count, queries, heads_here, HEAD_DIM).transpose(0, 2, 1, 3)
    key_rows = grouped[:, :, 1]
    value_rows = grouped[:, :, 2]

    def heads_first(part):
        part_rows = part.shape[1]
        return part.reshape(seq_count, part_rows, heads_here, HEAD_DIM).transpose(0, 2, 1, 3)

    def forward_step(running, arrived, first_row, live=True):
        row_max, denominator, numerator = running
        key_part, value_part = arrived
        part_rows = key_part.shape[1]
        key_four = heads_first(key_part)
        value_four = heads_first(value_part)
        allowed = jnp.logical_and(query_docs[:, :, None] == key_docs[:, None, :], live)[:, None]
        scores = (
            jnp.einsum("shqe,shke->shqk", query_heads, key_four, preferred_element_type=f32)
            * scale_factor
        )
        masked = jnp.where(allowed, scores, -1e30)
        new_max = jnp.maximum(row_max, jnp.max(masked, axis=-1))
        exponent = jnp.where(allowed, jnp.exp(scores - new_max[..., None]), 0.0)
        denominator = jnp.sum(exponent, axis=-1)
        numerator = jnp.einsum(
            "shqk,shke->shqe", exponent.astype(bf16), value_four, preferred_element_type=f32
        )
        return (new_max, denominator, numerator)

    start_state = (
        jnp.full((seq_count, heads_here, queries), -1e30, f32),
        jnp.zeros((seq_count, heads_here, queries), f32),
        jnp.zeros((seq_count, heads_here, queries, HEAD_DIM), f32),
    )
    row_max, denominator, numerator = forward_step(
        start_state,
        (
            lax.all_gather(key_rows, "blk", axis=1, tiled=True),
            lax.all_gather(value_rows, "blk", axis=1, tiled=True),
        ),
        jnp.int32(0),
    )
    attention = numerator / denominator[..., None]
    log_total = row_max + jnp.log(denominator)
    attn_send = (
        attention.astype(bf16).transpose(0, 2, 1, 3).reshape(seq_count, queries, local_width)
    )
    mixed = lax.all_to_all(attn_send, "head", split_axis=1, concat_axis=2, tiled=True)
    branch = jnp.einsum("std,de->ste", mixed, full_out, preferred_element_type=f32)
    hidden = residual + gate_attn * branch
    normed_two, inverse_two = normalize(hidden)
    scaled_two = normed_two * gain_two
    moved = (scaled_two * (1.0 + scale_mlp) + shift_mlp).astype(bf16)
    upper_in = jnp.einsum(
        "std,df->stf", moved, full_up, preferred_element_type=f32
    ) + full_up_bias.astype(f32)
    active = jax.nn.gelu(upper_in, approximate=True).astype(bf16)
    lower_out = jnp.einsum(
        "stf,fd->std", active, full_down, preferred_element_type=f32
    ) + full_down_bias.astype(f32)
    final_state = hidden + gate_mlp * lower_out
    mismatch = final_state - teacher.astype(f32)
    error_here = jnp.sum(mask_float[:, :, None] * mismatch * mismatch)
    error_all, count_all = lax.psum((error_here, count_here), ("head", "blk"))
    loss_value = error_all / (count_all * model_width)
    grad_final = seq_count * length / count_all * mask_float[:, :, None] * mismatch
    grad_lower = (gate_mlp * grad_final).astype(bf16)
    grad_gate_mlp = jnp.sum(grad_final * lower_out, axis=1)
    grad_down_weight = jnp.einsum("stf,std->fd", active, grad_lower, preferred_element_type=f32)
    grad_down_bias = jnp.sum(grad_lower.astype(f32), axis=(0, 1))
    grad_active = jnp.einsum("std,fd->stf", grad_lower, full_down, preferred_element_type=f32)
    unused_value, gelu_back = jax.vjp(partial(jax.nn.gelu, approximate=True), upper_in)
    grad_upper = gelu_back(grad_active)[0].astype(bf16)
    grad_up_weight = jnp.einsum("std,stf->df", moved, grad_upper, preferred_element_type=f32)
    grad_up_bias = jnp.sum(grad_upper.astype(f32), axis=(0, 1))
    grad_moved = jnp.einsum("stf,df->std", grad_upper, full_up, preferred_element_type=f32)
    grad_shift_mlp = jnp.sum(grad_moved, axis=1)
    grad_scale_mlp = jnp.sum(grad_moved * scaled_two, axis=1)
    grad_scaled_two = grad_moved * (1.0 + scale_mlp)
    grad_gain_mlp = jnp.sum(grad_scaled_two * normed_two, axis=(0, 1))
    grad_hidden = grad_final + norm_back(grad_scaled_two * gain_two, normed_two, inverse_two)
    grad_branch = (gate_attn * grad_hidden).astype(bf16)
    grad_gate_attn = jnp.sum(grad_hidden * branch, axis=1)
    grad_out_weight = jnp.einsum("ste,std->ed", mixed, grad_branch, preferred_element_type=f32)
    grad_mixed = jnp.einsum(
        "std,ed->ste", grad_branch, full_out, preferred_element_type=f32
    ).astype(bf16)
    grad_heads = lax.all_to_all(grad_mixed, "head", split_axis=2, concat_axis=1, tiled=True)
    grad_four = heads_first(grad_heads)
    row_delta = jnp.sum(grad_four.astype(f32) * attention, axis=-1)

    def query_step(running, arrived, first_row, live=True):
        key_part, value_part = arrived
        part_rows = key_part.shape[1]
        key_four = heads_first(key_part)
        value_four = heads_first(value_part)
        allowed = jnp.logical_and(query_docs[:, :, None] == key_docs[:, None, :], live)[:, None]
        scores = (
            jnp.einsum("shqe,shke->shqk", query_heads, key_four, preferred_element_type=f32)
            * scale_factor
        )
        probabilities = jnp.where(allowed, jnp.exp(scores - log_total[..., None]), 0.0)
        grad_probs = jnp.einsum(
            "shqe,shke->shqk", grad_four, value_four, preferred_element_type=f32
        )
        grad_scores = (probabilities * (grad_probs - row_delta[..., None])).astype(bf16)
        return (
            jnp.einsum("shqk,shke->shqe", grad_scores, key_four, preferred_element_type=f32)
            * scale_factor
        )

    key_local = heads_first(key_rows)
    value_local = heads_first(value_rows)

    def key_step(running, arrived, first_row, live=True):
        query_part, grad_part, stat_part = arrived
        part_rows = query_part.shape[1]
        query_low = heads_first(query_part)
        grad_low = heads_first(grad_part)
        stats = jnp.sum(
            stat_part.astype(f32).reshape(seq_count, part_rows, 2, 3, heads_here), axis=3
        )
        total_part = stats[:, :, 0].transpose(0, 2, 1)
        delta_part = stats[:, :, 1].transpose(0, 2, 1)
        allowed = jnp.logical_and(key_docs[:, :, None] == query_docs[:, None, :], live)[:, None]
        scores = (
            jnp.einsum("shqe,shke->shqk", query_low, key_local, preferred_element_type=f32)
            * scale_factor
        )
        probabilities = jnp.where(allowed, jnp.exp(scores - total_part[..., None]), 0.0)
        grad_probs = jnp.einsum(
            "shqe,shke->shqk", grad_low, value_local, preferred_element_type=f32
        )
        grad_scores = (probabilities * (grad_probs - delta_part[..., None])).astype(bf16)
        grad_value = jnp.einsum(
            "shqk,shqe->shke", probabilities.astype(bf16), grad_low, preferred_element_type=f32
        )
        grad_key = (
            jnp.einsum("shqk,shqe->shke", grad_scores, query_low, preferred_element_type=f32)
            * scale_factor
        )
        return (grad_key, grad_value)

    total_rows = log_total.transpose(0, 2, 1)
    delta_rows = row_delta.transpose(0, 2, 1)
    stat_send = jnp.stack([split_three(total_rows), split_three(delta_rows)], axis=2).reshape(
        seq_count, queries, 6 * heads_here
    )
    empty_grad = jnp.zeros((seq_count, heads_here, queries, HEAD_DIM), f32)
    grad_query = query_step(
        empty_grad,
        (
            lax.all_gather(key_rows, "blk", axis=1, tiled=True),
            lax.all_gather(value_rows, "blk", axis=1, tiled=True),
        ),
        jnp.int32(0),
    )
    grad_key, grad_value = key_step(
        (empty_grad, empty_grad),
        (
            lax.all_gather(query_send, "blk", axis=1, tiled=True),
            lax.all_gather(grad_heads, "blk", axis=1, tiled=True),
            lax.all_gather(stat_send, "blk", axis=1, tiled=True),
        ),
        jnp.int32(0),
    )

    def rows_first(value):
        return value.transpose(0, 2, 1, 3).reshape(seq_count, queries, local_width)

    grad_triple = jnp.stack(
        [rows_first(grad_query), rows_first(grad_key), rows_first(grad_value)], axis=2
    ).astype(bf16)
    grad_tokens = lax.all_to_all(grad_triple, "head", split_axis=1, concat_axis=3, tiled=True)
    grad_flat = grad_tokens.reshape(seq_count, tokens, 3 * model_width)
    grad_qkv_weight = jnp.einsum("std,stf->df", entered, grad_flat, preferred_element_type=f32)
    grad_entered = jnp.einsum("stf,df->std", grad_flat, full_qkv, preferred_element_type=f32)
    grad_shift_attn = jnp.sum(grad_entered, axis=1)
    grad_scale_attn = jnp.sum(grad_entered * scaled_one, axis=1)
    grad_scaled_one = grad_entered * (1.0 + scale_attn)
    grad_gain_attn = jnp.sum(grad_scaled_one * normed_one, axis=(0, 1))
    grad_input = grad_hidden + norm_back(grad_scaled_one * gain_one, normed_one, inverse_one)
    grad_modulation = jnp.stack(
        [
            grad_shift_attn,
            grad_scale_attn,
            grad_gate_attn,
            grad_shift_mlp,
            grad_scale_mlp,
            grad_gate_mlp,
        ],
        axis=1,
    ).reshape(seq_count, 6 * model_width)
    grad_ada_weight = jnp.dot(time_embed.T, grad_modulation, precision=precise)
    grad_ada_bias = jnp.sum(grad_modulation, axis=0)
    later_owned = (
        lax.psum_scatter(grad_out_weight, ("head", "blk"), scatter_dimension=0, tiled=True),
        lax.psum_scatter(grad_up_weight, ("head", "blk"), scatter_dimension=0, tiled=True),
        lax.psum_scatter(grad_down_weight, ("head", "blk"), scatter_dimension=0, tiled=True),
        lax.psum_scatter(grad_gain_mlp, ("head", "blk"), scatter_dimension=0, tiled=True),
        lax.psum_scatter(grad_up_bias, ("head", "blk"), scatter_dimension=0, tiled=True),
        lax.psum_scatter(grad_down_bias, ("head", "blk"), scatter_dimension=0, tiled=True),
    )
    shard_out, shard_up, shard_down, shard_gain_mlp, shard_up_bias, shard_down_bias = later_owned
    first_owned = (
        lax.psum_scatter(grad_qkv_weight, ("head", "blk"), scatter_dimension=0, tiled=True),
        lax.psum_scatter(grad_ada_weight, ("head", "blk"), scatter_dimension=1, tiled=True),
        lax.psum_scatter(grad_ada_bias, ("head", "blk"), scatter_dimension=0, tiled=True),
        lax.psum_scatter(grad_gain_attn, ("head", "blk"), scatter_dimension=0, tiled=True),
    )
    shard_qkv, shard_ada, shard_ada_bias, shard_gain_attn = first_owned
    return (
        final_state.astype(bf16),
        loss_value,
        grad_input,
        shard_ada,
        shard_ada_bias,
        shard_gain_attn,
        shard_qkv,
        shard_out,
        shard_gain_mlp,
        shard_up,
        shard_up_bias,
        shard_down,
        shard_down_bias,
    )


def solution(mesh):
    return jax.shard_map(
        on_device,
        mesh=mesh,
        in_specs=(
            P(None, ("blk", "head"), None),
            P(),
            P(None, ("blk", "head")),
            P(None, ("blk", "head")),
            P(None, ("blk", "head"), None),
            P(None, ("head", "blk")),
            P(("head", "blk")),
            P(("head", "blk")),
            P(("head", "blk"), None),
            P(("head", "blk"), None),
            P(("head", "blk")),
            P(("head", "blk"), None),
            P(("head", "blk")),
            P(("head", "blk"), None),
            P(("head", "blk")),
        ),
        out_specs=(
            P(None, ("blk", "head"), None),
            P(),
            P(None, ("blk", "head"), None),
            P(None, ("head", "blk")),
            P(("head", "blk")),
            P(("head", "blk")),
            P(("head", "blk"), None),
            P(("head", "blk"), None),
            P(("head", "blk")),
            P(("head", "blk"), None),
            P(("head", "blk")),
            P(("head", "blk"), None),
            P(("head", "blk")),
        ),
        check_vma=False,
    )
```

profile of v0, /device:TPU:0, one launch (start us, length us, event | category | flops | bytes accessed | tf_op | source)
XLA Modules:
  0.0 1162.7 jit_solution(6677036301440943555)
XLA Ops:
  13.0 42.4 %all-reduce.11 = (bf16[4608]{0:T(1024)(128)(2,1)S(1)}, bf16[768]{0:T(1024)(128)(2,1)S(1)}, bf16[768]{0:T(1024)(128)(2,1)S(1)}, bf16[3072]{0:T(1024)(128)(2,1)S(1)}, bf16[768]{0:T(1024)(128)(2,1)S(1)}) all-reduce(bf16[4608]{0:T(1024)(128)(2,1)S(1)} %dynamic-update-slice, ...), channel_id=1, replica_groups=mesh['head'=4,'blk'=8] {'head','blk'}, use_global_device_ids=true, to_apply=%add | all-reduce | flops 9984 | bytes 39936
  57.6 10.2 all-gather.14.cloned.1.call-done
  70.2 59.7 %all-gather.16.cloned.1.call-done = bf16[768,2304]{1,0:T(8,128)(2,1)} async-done(((bf16[24,2304]{1,0:T(8,128)(2,1)}), bf16[768,2304]{1,0:T(8,128)(2,1)}) %all-gather.16.cloned.1.call-update) | async-done | bytes 3538960 | tf_op jit(solution)/shard_map/all_gather | solution.py:72
  135.3 12.0 %all_to_all.69 = bf16[4,2,36864]{2,1,0:T(2,128)(2,1)S(1)} all-to-all(bf16[4,2,36864]{2,1,0:T(2,128)(2,1)S(1)} %reshape.208), channel_id=1, replica_groups=mesh['head'=4,'blk'=8] {'head'}, dimensions={0} | all-to-all | bytes 1179648 | tf_op jit(solution)/shard_map/all_to_all | solution.py:113
  154.6 39.7 %psum.15 = f32[]{:T(128)} all-reduce(f32[]{:T(128)} %convert_reduce_fusion.4), channel_id=1, replica_groups=mesh['head'=4,'blk'=8] {'head','blk'}, use_global_device_ids=true, to_apply=%region_9.10 | all-reduce | flops 1 | bytes 8 | tf_op jit(solution)/shard_map/psum | solution.py:177
  194.3 66.7 %all-gather.3 = s32[32,64,2]{1,2,0:T(2,128)S(1)} all-gather(s32[1,64,2]{1,2,0:T(2,128)S(1)} %bitcast.271), channel_id=1, replica_groups=mesh['head'=4,'blk'=8] {'head','blk'}, dimensions={0}, use_global_device_ids=true | all-gather | bytes 16896 | tf_op jit(solution)/shard_map/all_gather | solution.py:62
  265.8 4.4 copy.137
  270.2 5.9 select_reduce_fusion
  276.1 7.0 fusion
  283.1 7.0 fusion.75
  295.3 5.0 all-to-all-done.1
  300.8 5.0 all-gather.18.cloned.1.call-done
  308.4 62.9 %all-gather.20.cloned.1.call-done = bf16[768,3072]{1,0:T(8,128)(2,1)} async-done(((bf16[24,3072]{1,0:T(8,128)(2,1)}), bf16[768,3072]{1,0:T(8,128)(2,1)}) %all-gather.20.cloned.1.call-update) | async-done | bytes 4718608 | tf_op jit(solution)/shard_map/all_gather | solution.py:74
  374.6 62.2 %all-gather.22.cloned.1.call-done = bf16[3072,768]{1,0:T(8,128)(2,1)} async-done(((bf16[96,768]{1,0:T(8,128)(2,1)}), bf16[3072,768]{1,0:T(8,128)(2,1)}) %all-gather.22.cloned.1.call-update) | async-done | bytes 4718608 | tf_op jit(solution)/shard_map/all_gather | solution.py:75
  436.8 4.9 convert_reduce_fusion.2
  452.3 9.4 all_to_all.70
  470.2 17.1 %all-gather.30.cloned.1.call-done = bf16[2,2048,1,192]{3,1,2,0:T(8,128)(2,1)} async-done(((bf16[2,256,1,192]{3,1,2,0:T(8,128)(2,1)}), bf16[2,2048,1,192]{3,1,2,0:T(8,128)(2,1)}) %all-gather.30.cloned.1.call-update) | async-done | bytes 1572880 | tf_op jit(solution)/shard_map/all_gather | solution.py:274
  491.3 7.8 fusion.101
  504.7 12.0 %fusion.52 = bf16[2,3,256,64]{2,3,1,0:T(8,128)(2,1)} fusion(bf16[2,3,2048,64]{2,3,1,0:T(8,128)(2,1)} %bitcast.231, f32[2,3,256,2048]{3,2,1,0:T(8,128)} %get-tuple-element.63, f32[2,3,256]{2,1,0:T(4,128)S(1)} %multiply_reduce_fusion.4, f32[2,3,256]{2,1,0:T(4,128)S(1)} %log_add_fusion, pred[2,256,2048]{2,1,0:T(8,128)(4,1)S(1)} %broadcast_compare_fusion.1, ...), kind=kOutput, calls=%fused_computation.58 | convolution fusion | flops 824377344 | bytes 17182720 | tf_op jit(solution)/shard_map/shqk,shke->shqe/dot_general | solution.py:221
  517.9 20.8 %all_gather.64 = bf16[2,2048,18]{1,0,2:T(2,128)(2,1)S(1)} all-gather(bf16[2,256,18]{1,0,2:T(2,128)(2,1)S(1)} %bitcast.268), channel_id=1, replica_groups=mesh['head'=4,'blk'=8] {'blk'}, dimensions={1}, use_global_device_ids=true | all-gather | bytes 165888 | tf_op jit(solution)/shard_map/all_gather | solution.py:276
  544.2 11.6 fusion.53
  557.6 7.4 fusion.54
  568.3 14.2 %all_to_all.71 = bf16[2,256,3,192]{3,0,2,1:T(2,128)(2,1)S(1)} all-to-all(bf16[2,256,3,192]{3,0,2,1:T(2,128)(2,1)S(1)} %pad_maximum_fusion), channel_id=1, replica_groups=mesh['head'=4,'blk'=8] {'head'}, dimensions={1} | all-to-all | bytes 1179648 | tf_op jit(solution)/shard_map/all_to_all | solution.py:287
  584.0 4.7 fusion.72
  589.4 5.2 convolution_bitcast_fusion
  594.8 5.9 convolution_bitcast_fusion.2
  601.6 5.2 convolution_bitcast_fusion.1
  612.6 39.1 %all-reduce.10 = (f32[]{:T(128)}, f32[4608]{0:T(1024)S(1)}, f32[768]{0:T(1024)S(1)}, f32[768]{0:T(1024)S(1)}, f32[3072]{0:T(1024)S(1)}, /*index=5*/f32[768]{0:T(1024)S(1)}) all-reduce(f32[]{:T(128)} %get-tuple-element.47, f32[4608]{0:T(1024)S(1)} %reduce_sum.238, ...), channel_id=1, replica_groups=mesh['head'=4,'blk'=8] {'head','blk'}, use_global_device_ids=true, to_apply=%region_7.8 | all-reduce | flops 9985 | bytes 79880 | tf_op jit(solution)/shard_map/psum | solution.py:177
  656.4 91.1 %reduce-scatter.6.cloned.1.call-done = f32[128,144]{0,1:T(8,128)} async-done(((f32[128,4608]{0,1:T(8,128)}), f32[128,144]{0,1:T(8,128)}) %reduce-scatter.6.cloned.1.call-update) | async-done | bytes 73744 | tf_op jit(solution)/shard_map/reduce_scatter | solution.py:320
  747.4 140.9 %reduce-scatter.12.cloned.1.call-done = f32[24,3072]{1,0:T(8,128)} async-done(((f32[768,3072]{1,0:T(8,128)}), f32[24,3072]{1,0:T(8,128)}) %reduce-scatter.12.cloned.1.call-update) | async-done | bytes 294928 | tf_op jit(solution)/shard_map/reduce_scatter | solution.py:311
  888.3 142.2 %reduce-scatter.14.cloned.1.call-done = f32[96,768]{1,0:T(8,128)} async-done(((f32[3072,768]{1,0:T(8,128)}), f32[96,768]{1,0:T(8,128)}) %reduce-scatter.14.cloned.1.call-update) | async-done | bytes 294928 | tf_op jit(solution)/shard_map/reduce_scatter | solution.py:312
  1030.5 124.3 %reduce-scatter.8.cloned.1.call-done = f32[24,2304]{1,0:T(8,128)} async-done(((f32[768,2304]{1,0:T(8,128)}), f32[24,2304]{1,0:T(8,128)}) %reduce-scatter.8.cloned.1.call-update) | async-done | bytes 221200 | tf_op jit(solution)/shard_map/reduce_scatter | solution.py:319
  (250 shorter events, 90.4 us)
Async XLA Ops:
  7.2 60.6 %copy-start = (f32[2,128]{1,0:T(2,128)S(1)}, f32[2,128]{1,0:T(2,128)}, u32[]{:S(2)}) copy-start(f32[2,128]{1,0:T(2,128)} %param.16) | copy-start | bytes 3076
  7.2 122.7 %copy-start.1 = (bf16[2,64,768]{2,1,0:T(8,128)(2,1)S(1)}, bf16[2,64,768]{2,1,0:T(8,128)(2,1)}, u32[]{:S(2)}) copy-start(bf16[2,64,768]{2,1,0:T(8,128)(2,1)} %param.15) | copy-start | bytes 589828
  7.2 60.6 %all-gather.14.cloned.1.call-start = ((), (), s32[]{:S(2)}) async-start(), calls=%async_computation.9 | async-start | bytes 1216512 | tf_op jit(solution)/shard_map/all_gather | solution.py:76
  7.9 122.0 %all-gather.16.cloned.1.call-start = ((), (), s32[]{:S(2)}) async-start(), calls=%async_computation.10 | async-start | bytes 3649536 | tf_op jit(solution)/shard_map/all_gather | solution.py:72
  8.7 254.2 %all-gather.26.cloned.1.call-start = ((), (), s32[]{:S(2)}) async-start(), calls=%async_computation.20 | async-start | bytes 2359296 | tf_op jit(solution)/shard_map/all_gather | solution.py:151
  56.4 76.2 %copy-start.31 = (f32[2,64]{1,0:T(2,128)}, f32[2,64]{1,0:T(2,128)S(1)}, u32[]{:S(2)}) copy-start(f32[2,64]{1,0:T(2,128)S(1)} %broadcast_multiply_fusion.6) | copy-start | bytes 1540
  57.6 75.1 %copy-start.33 = (f32[2,64]{1,0:T(2,128)}, f32[2,64]{1,0:T(2,128)S(1)}, u32[]{:S(2)}) copy-start(f32[2,64]{1,0:T(2,128)S(1)} %add_rsqrt_fusion.1) | copy-start | bytes 1540
  70.2 62.4 %copy-start.24 = (f32[2,1,1,768]{3,0,1,2:T(2,128)}, f32[2,1,1,768]{3,0,1,2:T(2,128)S(1)}, u32[]{:S(2)}) copy-start(f32[2,1,1,768]{3,0,1,2:T(2,128)S(1)} %copy.171) | copy-start | bytes 18436
  70.2 62.4 %copy-start.26 = (f32[2,1,1,768]{3,0,1,2:T(2,128)}, f32[2,1,1,768]{3,0,1,2:T(2,128)S(1)}, u32[]{:S(2)}) copy-start(f32[2,1,1,768]{3,0,1,2:T(2,128)S(1)} %copy.170) | copy-start | bytes 18436
  150.4 43.8 %copy-start.46 = (s32[2,64]{1,0:T(2,128)S(1)}, s32[2,64]{1,0:T(2,128)}, u32[]{:S(2)}) copy-start(s32[2,64]{1,0:T(2,128)} %param.17) | copy-start | bytes 1540
  151.4 114.3 %copy-start.11 = (bf16[2,256,1,192]{3,1,2,0:T(8,128)(2,1)}, bf16[2,256,1,192]{3,1,2,0:T(8,128)(2,1)S(1)}, u32[]{:S(2)}) copy-start(bf16[2,256,1,192]{3,1,2,0:T(8,128)(2,1)S(1)} %get-tuple-element.46) | copy-start | bytes 589828
  151.5 114.3 %all-gather.28.cloned.1.call-start = ((), (), s32[]{:S(2)}) async-start(), calls=%async_computation.21 | async-start | bytes 2359296 | tf_op jit(solution)/shard_map/all_gather | solution.py:152
  152.0 153.8 %all-gather.18.cloned.1.call-start = ((), (), s32[]{:S(2)}) async-start(), calls=%async_computation.11 | async-start | bytes 1216512 | tf_op jit(solution)/shard_map/all_gather | solution.py:73
  152.6 218.7 %all-gather.20.cloned.1.call-start = ((), (), s32[]{:S(2)}) async-start(), calls=%async_computation.12 | async-start | bytes 4866048 | tf_op jit(solution)/shard_map/all_gather | solution.py:74
  153.2 283.6 %all-gather.22.cloned.1.call-start = ((), (), s32[]{:S(2)}) async-start(), calls=%async_computation.13 | async-start | bytes 4866048 | tf_op jit(solution)/shard_map/all_gather | solution.py:75
  290.9 9.4 all-to-all-start.1
  294.3 193.0 %all-gather.30.cloned.1.call-start = ((), (), s32[]{:S(2)}) async-start(), calls=%async_computation.22 | async-start | bytes 2359296 | tf_op jit(solution)/shard_map/all_gather | solution.py:274
  294.4 77.0 %copy-start.28 = (f32[2,768]{1,0:T(2,128)}, f32[2,768]{1,0:T(2,128)S(1)}, u32[]{:S(2)}) copy-start(f32[2,768]{1,0:T(2,128)S(1)} %get-tuple-element.72) | copy-start | bytes 18436
  294.4 152.3 %copy-start.19 = (f32[2,768]{1,0:T(2,128)}, f32[2,768]{1,0:T(2,128)S(1)}, u32[]{:S(2)}) copy-start(f32[2,768]{1,0:T(2,128)S(1)} %get-tuple-element.73) | copy-start | bytes 18436
  295.1 245.2 %all-gather.24.cloned.1.call-start = ((), (), s32[]{:S(2)}) async-start(), calls=%async_computation.14 | async-start | bytes 2359296 | tf_op jit(solution)/shard_map/all_gather | solution.py:275
  300.8 70.5 %copy-start.12 = (bf16[2,64,768]{2,1,0:T(8,128)(2,1)}, bf16[2,64,768]{2,1,0:T(8,128)(2,1)S(1)}, u32[]{:S(2)}) copy-start(bf16[2,64,768]{2,1,0:T(8,128)(2,1)S(1)} %all_to_all.57) | copy-start | bytes 589828
  308.4 138.4 %copy-start.29 = (f32[2,64]{1,0:T(2,128)}, f32[2,64]{1,0:T(2,128)S(1)}, u32[]{:S(2)}) copy-start(f32[2,64]{1,0:T(2,128)S(1)} %add_rsqrt_fusion) | copy-start | bytes 1540
  465.5 190.9 %reduce-scatter.10.cloned.1.call-start = ((), (), s32[]{:S(2)}) async-start(), calls=%async_computation.17 | async-start | bytes 2433024 | tf_op jit(solution)/shard_map/reduce_scatter | solution.py:310
  470.2 21.0 %copy-start.17 = (bf16[2,256,1,192]{1,3,0,2:T(8,128)(2,1)S(1)}, bf16[2,256,1,192]{1,3,0,2:T(8,128)(2,1)}, u32[]{:S(2)}) copy-start(bf16[2,256,1,192]{1,3,0,2:T(8,128)(2,1)} %copy.145) | copy-start | bytes 589828
  501.0 246.4 %reduce-scatter.6.cloned.1.call-start = ((), (), s32[]{:S(2)}) async-start(), calls=%async_computation.15 | async-start | bytes 2433024 | tf_op jit(solution)/shard_map/reduce_scatter | solution.py:320
  594.7 293.6 %reduce-scatter.12.cloned.1.call-start = ((), (), s32[]{:S(2)}) async-start(), calls=%async_computation.18 | async-start | bytes 9732096 | tf_op jit(solution)/shard_map/reduce_scatter | solution.py:311
  600.7 429.8 %reduce-scatter.14.cloned.1.call-start = ((), (), s32[]{:S(2)}) async-start(), calls=%async_computation.19 | async-start | bytes 9732096 | tf_op jit(solution)/shard_map/reduce_scatter | solution.py:312
  606.8 548.0 %reduce-scatter.8.cloned.1.call-start = ((), (), s32[]{:S(2)}) async-start(), calls=%async_computation.16 | async-start | bytes 7299072 | tf_op jit(solution)/shard_map/reduce_scatter | solution.py:319
  611.7 43.7 %copy-start.48 = (f32[2,64]{1,0:T(2,128)S(1)}, f32[2,64]{1,0:T(2,128)}, u32[]{:S(2)}) copy-start(f32[2,64]{1,0:T(2,128)} %get-tuple-element.17) | copy-start | bytes 1540
  611.7 43.7 %copy-start.47 = (f32[2,64]{1,0:T(2,128)S(1)}, f32[2,64]{1,0:T(2,128)}, u32[]{:S(2)}) copy-start(f32[2,64]{1,0:T(2,128)} %get-tuple-element.19) | copy-start | bytes 1540
  611.7 43.7 %copy-start.5 = (f32[2,64,768]{2,1,0:T(8,128)S(1)}, f32[2,64,768]{2,1,0:T(8,128)}, u32[]{:S(2)}) copy-start(f32[2,64,768]{2,1,0:T(8,128)} %copy-done.3) | copy-start | bytes 1179652
  611.7 43.7 %copy-start.18 = (f32[2,64,768]{2,1,0:T(8,128)S(1)}, f32[2,64,768]{2,1,0:T(8,128)}, u32[]{:S(2)}) copy-start(f32[2,64,768]{2,1,0:T(8,128)} %get-tuple-element.69) | copy-start | bytes 1179652
  (35 other events, 146.3 us)
Sparse Core Ops, SparseCore 0:
  11.0 56.8 all-gather.13
  70.7 59.1 all-gather.15
  151.6 47.5 all-gather.25
  201.8 48.6 all-gather.27
  253.3 52.5 all-gather.17
  308.6 62.6 all-gather.19
  374.3 62.4 all-gather.21
  439.0 48.3 all-gather.29
  489.5 49.7 all-gather.23
  545.0 97.6 reduce-scatter.9
  649.4 97.9 reduce-scatter.5
  753.8 134.5 reduce-scatter.11
  895.8 134.6 reduce-scatter.13
  1036.6 118.1 reduce-scatter.7
where the time goes:
time: 1170 us; the launch traced here: 1160 us
  waiting for transfers between devices  725 us (62%)
  blocking collectives  244 us (21%)
  matrix products  99.8 us (9%)
  local copies, waits for them, and re-layouts  52.4 us (4%)
  other arithmetic  18.4 us (2%)
  between operations  18.2 us (2%)
    reduce_scatter x1, waiting for transfers between devices, on_device(): lax.psum_scatter(grad_down_weight, ('head', 'blk'), scatter_dimension=0,...  142 us
    reduce_scatter x1, waiting for transfers between devices, on_device(): lax.psum_scatter(grad_up_weight, ('head', 'blk'), scatter_dimension=0, ti...  141 us
    reduce_scatter x1, waiting for transfers between devices, on_device(): lax.psum_scatter(grad_qkv_weight, ('head', 'blk'), scatter_dimension=0, t...  124 us
    reduce_scatter x1, waiting for transfers between devices, on_device(): lax.psum_scatter(grad_ada_weight, ('head', 'blk'), scatter_dimension=1, t...  91.1 us
    psum x2, blocking collectives, on_device(): error_all, count_all = lax.psum((error_here, count_here), ('head', 'blk'))  78.8 us
    all_gather x1, blocking collectives, on_device(): all_docs = lax.all_gather(segments, ('head', 'blk'), axis=1, tiled=True)  66.7 us
    all_gather x1, waiting for transfers between devices, on_device(): lax.all_gather(up_weight, ('head', 'blk'), axis=0, tiled=True)  62.9 us
    all_gather x1, waiting for transfers between devices, on_device(): lax.all_gather(down_weight, ('head', 'blk'), axis=0, tiled=True)  62.2 us
  transfers between devices with their start and end apart: 15, of which 11 were waited for; matrix products, arithmetic and copies ran while one was open for 14% of the time, Pallas kernels for 0%

commit v1 on v0

--- a/solution.py
+++ b/solution.py
@@ -7,6 +7,18 @@
 HEADS = 12
 HEAD_DIM = 64
 precise = lax.Precision.HIGHEST
+
+
+def collect(value, axis, dim):
+    ways, here, step = (lax.axis_size(axis), lax.axis_index(axis), value.shape[dim])
+    line, have = (value, 1)
+    while have < ways:
+        line = jnp.concatenate(
+            [line, lax.ppermute(line, axis, [(d, (d - have) % ways) for d in range(ways)])],
+            axis=dim,
+        )
+        have = 2 * have
+    return jnp.roll(line, here * step, axis=dim)
 
 
 def normalize(hidden):
@@ -69,7 +81,7 @@
     mask_float = valid_mask.astype(f32)
     count_here = jnp.sum(mask_float)
     gathered = (
-        lax.all_gather(qkv_weight, ("head", "blk"), axis=0, tiled=True),
+        collect(qkv_weight, ("head", "blk"), 0),
         lax.all_gather(out_weight, ("head", "blk"), axis=0, tiled=True),
         lax.all_gather(up_weight, ("head", "blk"), axis=0, tiled=True),
         lax.all_gather(down_weight, ("head", "blk"), axis=0, tiled=True),

time: 1170 us -> 1190 us (1.017)
  waiting for transfers between devices: 725 us -> 688 us
  blocking collectives: 244 us -> 277 us
  local copies, waits for them, and re-layouts: 52.4 us -> 69.6 us
    all_gather x1 -> x0, waiting for transfers between devices: 59.7 us -> none  [on_device(): lax.all_gather(qkv_weight, ('head', 'blk'), axis=0, tiled=True)]
    ppermute x0 -> x5, waiting for transfers between devices: none -> 39 us  [collect(): lax.ppermute(line, axis, [(d, (d - have) % ways) for d in range(ways)])]
    unnamed x1, blocking collectives: 42.4 us -> 77.1 us
  transfers between devices with their start and end apart: 15 -> 19, of which waited for: 11 -> 13; matrix products, arithmetic and copies ran while one was open for 14% -> 14% of each run, Pallas kernels for 0% -> 0%
where the time goes in v1:
time: 1190 us
  waiting for transfers between devices  688 us (58%)
  blocking collectives  277 us (23%)
  matrix products  99.7 us (8%)
  local copies, waits for them, and re-layouts  69.6 us (6%)
  other arithmetic  20.6 us (2%)
  between operations  18 us (2%)
  starting transfers between devices  13.3 us (1%)
    reduce_scatter x1, waiting for transfers between devices, on_device(): lax.psum_scatter(grad_down_weight, ('head', 'blk'), scatter_dimension=0,...  142 us
    reduce_scatter x1, waiting for transfers between devices, on_device(): lax.psum_scatter(grad_up_weight, ('head', 'blk'), scatter_dimension=0, ti...  141 us
    reduce_scatter x1, waiting for transfers between devices, on_device(): lax.psum_scatter(grad_qkv_weight, ('head', 'blk'), scatter_dimension=0, t...  124 us
    reduce_scatter x1, waiting for transfers between devices, on_device(): lax.psum_scatter(grad_ada_weight, ('head', 'blk'), scatter_dimension=1, t...  86.9 us
    unnamed x1, blocking collectives  77.1 us
    psum x2, blocking collectives, on_device(): error_all, count_all = lax.psum((error_here, count_here), ('head', 'blk'))  76.7 us
    all_gather x1, blocking collectives, on_device(): all_docs = lax.all_gather(segments, ('head', 'blk'), axis=1, tiled=True)  66.7 us
    all_gather x1, waiting for transfers between devices, on_device(): lax.all_gather(up_weight, ('head', 'blk'), axis=0, tiled=True)  62.9 us
  transfers between devices with their start and end apart: 19, of which 13 were waited for; matrix products, arithmetic and copies ran while one was open for 14% of the time, Pallas kernels for 0%

profile of v1, /device:TPU:0, one launch (start us, length us, event | category | flops | bytes accessed | tf_op | source)
XLA Modules:
  0.0 1186.8 jit_solution(13346700153040810410)
XLA Ops:
  7.2 6.4 collective-permute-start
  17.8 6.2 collective-permute-done.1
  26.7 20.8 %collective-permute-done.2 = bf16[96,2304]{1,0:T(8,128)(2,1)S(1)} collective-permute-done((bf16[96,2304]{1,0:T(8,128)(2,1)S(1)}, bf16[96,2304]{1,0:T(8,128)(2,1)S(1)}, u32[]{:S(2)}, u32[]{:S(2)}) %collective-permute-start.2) | collective-permute-done | bytes 442400 | tf_op jit(solution)/shard_map/ppermute | solution.py:17
  51.8 9.1 collective-permute-done.3
  65.0 77.1 %all-reduce.11 = (bf16[4608]{0:T(1024)(128)(2,1)S(1)}, bf16[768]{0:T(1024)(128)(2,1)S(1)}, bf16[768]{0:T(1024)(128)(2,1)S(1)}, bf16[3072]{0:T(1024)(128)(2,1)S(1)}, bf16[768]{0:T(1024)(128)(2,1)S(1)}) all-reduce(bf16[4608]{0:T(1024)(128)(2,1)S(1)} %dynamic-update-slice, ...), channel_id=1, replica_groups=mesh['head'=4,'blk'=8] {'head','blk'}, use_global_device_ids=true, to_apply=%add | all-reduce | flops 9984 | bytes 39936
  158.5 12.9 %all_to_all.69 = bf16[4,2,36864]{2,1,0:T(2,128)(2,1)S(1)} all-to-all(bf16[4,2,36864]{2,1,0:T(2,128)(2,1)S(1)} %reshape.208), channel_id=1, replica_groups=mesh['head'=4,'blk'=8] {'head'}, dimensions={0} | all-to-all | bytes 1179648 | tf_op jit(solution)/shard_map/all_to_all | solution.py:125
  178.6 38.9 %psum.15 = f32[]{:T(128)} all-reduce(f32[]{:T(128)} %convert_reduce_fusion.4), channel_id=1, replica_groups=mesh['head'=4,'blk'=8] {'head','blk'}, use_global_device_ids=true, to_apply=%region_9.10 | all-reduce | flops 1 | bytes 8 | tf_op jit(solution)/shard_map/psum | solution.py:189
  218.1 66.7 %all-gather.3 = s32[32,64,2]{1,2,0:T(2,128)S(1)} all-gather(s32[1,64,2]{1,2,0:T(2,128)S(1)} %bitcast.271), channel_id=1, replica_groups=mesh['head'=4,'blk'=8] {'head','blk'}, dimensions={0}, use_global_device_ids=true | all-gather | bytes 16896 | tf_op jit(solution)/shard_map/all_gather | solution.py:74
  294.1 5.9 select_reduce_fusion
  300.0 7.0 fusion
  307.0 6.9 fusion.77
  319.3 5.1 all-to-all-done.1
  324.9 6.1 all-gather.15.cloned.1.call-done
  333.6 62.9 %all-gather.17.cloned.1.call-done = bf16[768,3072]{1,0:T(8,128)(2,1)} async-done(((bf16[24,3072]{1,0:T(8,128)(2,1)}), bf16[768,3072]{1,0:T(8,128)(2,1)}) %all-gather.17.cloned.1.call-update) | async-done | bytes 4718608 | tf_op jit(solution)/shard_map/all_gather | solution.py:86
  399.7 62.0 %all-gather.19.cloned.1.call-done = bf16[3072,768]{1,0:T(8,128)(2,1)} async-done(((bf16[96,768]{1,0:T(8,128)(2,1)}), bf16[3072,768]{1,0:T(8,128)(2,1)}) %all-gather.19.cloned.1.call-update) | async-done | bytes 4718608 | tf_op jit(solution)/shard_map/all_gather | solution.py:87
  461.8 4.9 convert_reduce_fusion.2
  477.4 9.4 all_to_all.70
  496.5 15.6 %all-gather.27.cloned.1.call-done = bf16[2,2048,1,192]{3,1,2,0:T(8,128)(2,1)} async-done(((bf16[2,256,1,192]{3,1,2,0:T(8,128)(2,1)}), bf16[2,2048,1,192]{3,1,2,0:T(8,128)(2,1)}) %all-gather.27.cloned.1.call-update) | async-done | bytes 1572880 | tf_op jit(solution)/shard_map/all_gather | solution.py:286
  516.6 7.8 fusion.105
  531.5 20.2 %all_gather.60 = bf16[2,2048,18]{1,0,2:T(2,128)(2,1)S(1)} all-gather(bf16[2,256,18]{1,0,2:T(2,128)(2,1)S(1)} %bitcast.262), channel_id=1, replica_groups=mesh['head'=4,'blk'=8] {'blk'}, dimensions={1}, use_global_device_ids=true | all-gather | bytes 165888 | tf_op jit(solution)/shard_map/all_gather | solution.py:288
  553.1 12.1 %fusion.54 = bf16[2,3,256,64]{2,3,1,0:T(8,128)(2,1)} fusion(bf16[2,3,2048,64]{2,3,1,0:T(8,128)(2,1)} %bitcast.231, f32[2,3,256,2048]{3,2,1,0:T(8,128)} %get-tuple-element.73, f32[2,3,256]{2,1,0:T(4,128)S(1)} %multiply_reduce_fusion.4, f32[2,3,256]{2,1,0:T(4,128)} %log_add_fusion, pred[2,256,2048]{2,1,0:T(8,128)(4,1)S(1)} %broadcast_compare_fusion.1, ...), kind=kOutput, calls=%fused_computation.60 | convolution fusion | flops 824377344 | bytes 17182720 | tf_op jit(solution)/shard_map/shqk,shke->shqe/dot_general | solution.py:233
  571.1 7.4 fusion.56
  580.2 11.7 fusion.55
  596.1 14.5 %all_to_all.71 = bf16[2,256,3,192]{3,0,2,1:T(2,128)(2,1)S(1)} all-to-all(bf16[2,256,3,192]{3,0,2,1:T(2,128)(2,1)S(1)} %pad_maximum_fusion.1), channel_id=1, replica_groups=mesh['head'=4,'blk'=8] {'head'}, dimensions={1} | all-to-all | bytes 1179648 | tf_op jit(solution)/shard_map/all_to_all | solution.py:299
  619.5 5.3 convolution_bitcast_fusion
  624.9 5.1 convolution_bitcast_fusion.2
  631.0 5.2 convolution_bitcast_fusion.1
  642.2 37.8 %all-reduce.10 = (f32[]{:T(128)}, f32[4608]{0:T(1024)S(1)}, f32[768]{0:T(1024)S(1)}, f32[768]{0:T(1024)S(1)}, f32[3072]{0:T(1024)S(1)}, /*index=5*/f32[768]{0:T(1024)S(1)}) all-reduce(f32[]{:T(128)} %get-tuple-element.51, f32[4608]{0:T(1024)S(1)} %reduce_sum.238, ...), channel_id=1, replica_groups=mesh['head'=4,'blk'=8] {'head','blk'}, use_global_device_ids=true, to_apply=%region_7.8 | all-reduce | flops 9985 | bytes 79880 | tf_op jit(solution)/shard_map/psum | solution.py:189
  684.6 86.9 %reduce-scatter.6.cloned.1.call-done = f32[128,144]{0,1:T(8,128)} async-done(((f32[128,4608]{0,1:T(8,128)}), f32[128,144]{0,1:T(8,128)}) %reduce-scatter.6.cloned.1.call-update) | async-done | bytes 73744 | tf_op jit(solution)/shard_map/reduce_scatter | solution.py:332
  771.4 141.2 %reduce-scatter.12.cloned.1.call-done = f32[24,3072]{1,0:T(8,128)} async-done(((f32[768,3072]{1,0:T(8,128)}), f32[24,3072]{1,0:T(8,128)}) %reduce-scatter.12.cloned.1.call-update) | async-done | bytes 294928 | tf_op jit(solution)/shard_map/reduce_scatter | solution.py:323
  912.7 141.8 %reduce-scatter.14.cloned.1.call-done = f32[96,768]{1,0:T(8,128)} async-done(((f32[3072,768]{1,0:T(8,128)}), f32[96,768]{1,0:T(8,128)}) %reduce-scatter.14.cloned.1.call-update) | async-done | bytes 294928 | tf_op jit(solution)/shard_map/reduce_scatter | solution.py:324
  1054.4 124.5 %reduce-scatter.8.cloned.1.call-done = f32[24,2304]{1,0:T(8,128)} async-done(((f32[768,2304]{1,0:T(8,128)}), f32[24,2304]{1,0:T(8,128)}) %reduce-scatter.8.cloned.1.call-update) | async-done | bytes 221200 | tf_op jit(solution)/shard_map/reduce_scatter | solution.py:331
  (240 shorter events, 123.4 us)
Async XLA Ops:
  7.2 135.4 %copy-start = (f32[2,128]{1,0:T(2,128)S(1)}, f32[2,128]{1,0:T(2,128)}, u32[]{:S(2)}) copy-start(f32[2,128]{1,0:T(2,128)} %param.16) | copy-start | bytes 3076
  7.2 135.3 %all-gather.13.cloned.1.call-start = ((), (), s32[]{:S(2)}) async-start(), calls=%async_computation.9 | async-start | bytes 1216512 | tf_op jit(solution)/shard_map/all_gather | solution.py:88
  7.2 9.3 collective-permute-start
  17.4 6.6 collective-permute-start.1
  24.9 22.6 %collective-permute-start.2 = (bf16[96,2304]{1,0:T(8,128)(2,1)S(1)}, bf16[96,2304]{1,0:T(8,128)(2,1)S(1)}, u32[]{:S(2)}, u32[]{:S(2)}) collective-permute-start(bf16[96,2304]{1,0:T(8,128)(2,1)S(1)} %pad_maximum_fusion.2), channel_id=1, source_target_pairs={{0,28},{1,29},{2,30},{3,31},{4,0},{5,1},{6,2},{7,3},{8,4},{9,5},{1... | collective-permute-start | bytes 1327112 | tf_op jit(solution)/shard_map/ppermute | solution.py:17
  25.0 261.7 %all-gather.23.cloned.1.call-start = ((), (), s32[]{:S(2)}) async-start(), calls=%async_computation.19 | async-start | bytes 2359296 | tf_op jit(solution)/shard_map/all_gather | solution.py:163
  26.6 37.4 %copy-start.30 = (bf16[24]{0:T(256)(128)(2,1)S(1)}, bf16[24]{0:T(256)(128)(2,1)}, u32[]{:S(2)}) copy-start(bf16[24]{0:T(256)(128)(2,1)} %param.29) | copy-start | bytes 148
  26.6 37.6 %copy-start.31 = (bf16[24]{0:T(256)(128)(2,1)S(1)}, bf16[24]{0:T(256)(128)(2,1)}, u32[]{:S(2)}) copy-start(bf16[24]{0:T(256)(128)(2,1)} %param.25) | copy-start | bytes 148
  26.6 37.9 %copy-start.32 = (bf16[144]{0:T(256)(128)(2,1)S(1)}, bf16[144]{0:T(256)(128)(2,1)}, u32[]{:S(2)}) copy-start(bf16[144]{0:T(256)(128)(2,1)} %param.21) | copy-start | bytes 868
  26.7 38.1 %copy-start.33 = (bf16[96]{0:T(256)(128)(2,1)S(1)}, bf16[96]{0:T(256)(128)(2,1)}, u32[]{:S(2)}) copy-start(bf16[96]{0:T(256)(128)(2,1)} %param.27) | copy-start | bytes 580
  26.7 115.5 %copy-start.2 = (bf16[2,64,768]{2,1,0:T(8,128)(2,1)S(1)}, bf16[2,64,768]{2,1,0:T(8,128)(2,1)}, u32[]{:S(2)}) copy-start(bf16[2,64,768]{2,1,0:T(8,128)(2,1)} %param.15) | copy-start | bytes 589828
  48.5 12.5 %collective-permute-start.3 = (bf16[192,2304]{1,0:T(8,128)(2,1)S(1)}, bf16[192,2304]{1,0:T(8,128)(2,1)S(1)}, u32[]{:S(2)}, u32[]{:S(2)}) collective-permute-start(bf16[192,2304]{1,0:T(8,128)(2,1)S(1)} %pad_maximum_fusion), channel_id=1, source_target_pairs={{0,24},{1,25},{2,26},{3,27},{4,28},{5,29},{6,30},{7,31},{8,0},{9,1... | collective-permute-start | bytes 2654216 | tf_op jit(solution)/shard_map/ppermute | solution.py:17
  62.4 83.9 %copy-start.8 = (bf16[24,2304]{1,0:T(8,128)(2,1)S(1)}, bf16[24,2304]{1,0:T(8,128)(2,1)}, u32[]{:S(2)}) copy-start(bf16[24,2304]{1,0:T(8,128)(2,1)} %param.23) | copy-start | bytes 331780
  62.4 82.5 %collective-permute-start.4 = (bf16[384,2304]{1,0:T(8,128)(2,1)}, bf16[384,2304]{1,0:T(8,128)(2,1)S(1)}, u32[]{:S(2)}, u32[]{:S(2)}) collective-permute-start(bf16[384,2304]{1,0:T(8,128)(2,1)} %get-tuple-element.43), channel_id=1, source_target_pairs={{0,16},{1,17},{2,18},{3,19},{4,20},{5,21},{6,22},{7,23},{8,24},{9,... | collective-permute-start | bytes 5308424 | tf_op jit(solution)/shard_map/ppermute | solution.py:17
  172.2 45.9 %copy-start.26 = (s32[2,64]{1,0:T(2,128)S(1)}, s32[2,64]{1,0:T(2,128)}, u32[]{:S(2)}) copy-start(s32[2,64]{1,0:T(2,128)} %param.17) | copy-start | bytes 1540
  175.5 114.0 %copy-start.11 = (bf16[2,256,1,192]{3,1,2,0:T(8,128)(2,1)}, bf16[2,256,1,192]{3,1,2,0:T(8,128)(2,1)S(1)}, u32[]{:S(2)}) copy-start(bf16[2,256,1,192]{3,1,2,0:T(8,128)(2,1)S(1)} %get-tuple-element.48) | copy-start | bytes 589828
  175.5 114.0 %all-gather.25.cloned.1.call-start = ((), (), s32[]{:S(2)}) async-start(), calls=%async_computation.20 | async-start | bytes 2359296 | tf_op jit(solution)/shard_map/all_gather | solution.py:164
  176.3 154.7 %all-gather.15.cloned.1.call-start = ((), (), s32[]{:S(2)}) async-start(), calls=%async_computation.10 | async-start | bytes 1216512 | tf_op jit(solution)/shard_map/all_gather | solution.py:85
  176.9 219.6 %all-gather.17.cloned.1.call-start = ((), (), s32[]{:S(2)}) async-start(), calls=%async_computation.11 | async-start | bytes 4866048 | tf_op jit(solution)/shard_map/all_gather | solution.py:86
  177.4 284.3 %all-gather.19.cloned.1.call-start = ((), (), s32[]{:S(2)}) async-start(), calls=%async_computation.12 | async-start | bytes 4866048 | tf_op jit(solution)/shard_map/all_gather | solution.py:87
  285.8 175.9 %copy-start.22 = (f32[2,64]{1,0:T(2,128)}, f32[2,64]{1,0:T(2,128)S(1)}, u32[]{:S(2)}) copy-start(f32[2,64]{1,0:T(2,128)S(1)} %broadcast_multiply_fusion) | copy-start | bytes 1540
  314.8 9.6 all-to-all-start.1
  318.3 193.8 %all-gather.27.cloned.1.call-start = ((), (), s32[]{:S(2)}) async-start(), calls=%async_computation.21 | async-start | bytes 2359296 | tf_op jit(solution)/shard_map/all_gather | solution.py:286
  319.0 248.1 %all-gather.21.cloned.1.call-start = ((), (), s32[]{:S(2)}) async-start(), calls=%async_computation.13 | async-start | bytes 2359296 | tf_op jit(solution)/shard_map/all_gather | solution.py:287
  324.9 71.6 %copy-start.12 = (bf16[2,64,768]{2,1,0:T(8,128)(2,1)}, bf16[2,64,768]{2,1,0:T(8,128)(2,1)S(1)}, u32[]{:S(2)}) copy-start(bf16[2,64,768]{2,1,0:T(8,128)(2,1)S(1)} %all_to_all.57) | copy-start | bytes 589828
  396.5 65.3 %copy-start.28 = (bf16[2,64,768]{2,1,0:T(8,128)(2,1)S(1)}, bf16[2,64,768]{2,1,0:T(8,128)(2,1)}, u32[]{:S(2)}) copy-start(bf16[2,64,768]{2,1,0:T(8,128)(2,1)} %param.19) | copy-start | bytes 589828
  490.8 193.8 %reduce-scatter.10.cloned.1.call-start = ((), (), s32[]{:S(2)}) async-start(), calls=%async_computation.16 | async-start | bytes 2433024 | tf_op jit(solution)/shard_map/reduce_scatter | solution.py:322
  526.2 245.2 %reduce-scatter.6.cloned.1.call-start = ((), (), s32[]{:S(2)}) async-start(), calls=%async_computation.14 | async-start | bytes 2433024 | tf_op jit(solution)/shard_map/reduce_scatter | solution.py:332
  624.8 287.8 %reduce-scatter.12.cloned.1.call-start = ((), (), s32[]{:S(2)}) async-start(), calls=%async_computation.17 | async-start | bytes 9732096 | tf_op jit(solution)/shard_map/reduce_scatter | solution.py:323
  630.1 424.4 %reduce-scatter.14.cloned.1.call-start = ((), (), s32[]{:S(2)}) async-start(), calls=%async_computation.18 | async-start | bytes 9732096 | tf_op jit(solution)/shard_map/reduce_scatter | solution.py:324
  636.2 542.7 %reduce-scatter.8.cloned.1.call-start = ((), (), s32[]{:S(2)}) async-start(), calls=%async_computation.15 | async-start | bytes 7299072 | tf_op jit(solution)/shard_map/reduce_scatter | solution.py:331
  641.4 42.2 %copy-start.17 = (f32[2,64,768]{2,1,0:T(8,128)S(1)}, f32[2,64,768]{2,1,0:T(8,128)}, u32[]{:S(2)}) copy-start(f32[2,64,768]{2,1,0:T(8,128)} %get-tuple-element.79) | copy-start | bytes 1179652
  (23 other events, 132.7 us)
Sparse Core Ops, SparseCore 0:
  25.1 62.6 all-gather.12
  175.7 48.1 all-gather.22
  226.6 48.9 all-gather.24
  278.4 52.5 all-gather.14
  333.8 62.6 all-gather.16
  399.2 62.4 all-gather.18
  463.9 48.0 all-gather.26
  514.2 48.1 all-gather.20
  568.3 98.4 reduce-scatter.9
  673.3 98.0 reduce-scatter.5
  777.9 134.7 reduce-scatter.11
  920.0 134.3 reduce-scatter.13
  1060.7 118.1 reduce-scatter.7
